TPU v7x, 256 devices: a whole 4x4x8 slice. The times are simulated.
256 devices in a mesh: panel: 16 (over x, y), front: 16 (over z, core).
Axes of the slice: x: 4, y: 4, z: 8, core: 2. Of those that a mesh axis runs over, the one named last changes fastest.
Arguments:
- leaf_inv: float32 [16, 16, 768, 768], P('panel', 'front'), may hold values from -0.21875 to 0.21875
- parent_inv: float32 [16, 16, 768, 768], P('panel', 'front'), may hold values from -0.21875 to 0.21875
- up_coupling: float32 [16, 16, 384, 768], P('panel', 'front'), may hold values from -0.21875 to 0.21875
- down_coupling: float32 [16, 16, 768, 384], P('panel', 'front'), may hold values from -0.3125 to 0.3125
- interface_coupling: float32 [16, 16, 768, 512], P('panel', 'front'), may hold values from -0.25 to 0.25
- leaf_sources: float32 [16, 16, 3, 768, 128], P('panel', 'front'), may hold values from -6 to 6
- parent_sources: float32 [16, 16, 3, 768, 128], P('panel', 'front'), may hold values from -6 to 6
- parent_of: int32 [16, 16], P('panel'), may hold values from 0 to 15
- update_count: int32 [16, 16], P('panel'), may hold values from 128 to 384, as said below
- update_rows: int32 [16, 16, 384], P('panel'), may hold values from 0 to 767, as said below
Outputs:
- leaf_solution: float32 [16, 16, 3, 768, 128], P('panel', 'front')
- parent_solution: float32 [16, 16, 3, 768, 128], P('panel', 'front')
Inputs may be any that keep to these rules, and one draw needn't show every extreme that they name: `update_count`: a multiple of 128; some leaf of every panel has 384. `update_rows`: the entries of one leaf are distinct; those at or past its update_count are padding.
All inputs are finite; a program needn't handle non-finite values.
Results may differ from a plain program's by a relative error of at most 0.0003.
Values sent between devices are 32-bit elements; how exact they have to be, the bound alone decides.
A program may use at most 128 MiB of HBM per device.

v0:
```python
import jax
import jax.numpy as jnp
from jax import lax
from jax.sharding import PartitionSpec as P

TICKS = 3


highest_precision = lax.Precision.HIGHEST


def passed_along(value, axis, steps):
    count = lax.axis_size(axis)
    leading, last = (max(0, -steps), min(count, count - steps))
    return lax.ppermute(value, axis, [(source, source + steps) for source in range(leading, last)])


def product(matrix, operand):
    return jnp.dot(matrix, operand, precision=highest_precision, preferred_element_type=jnp.float32)


def local(
    leaf_inv,
    parent_inv,
    up_coupling,
    down_coupling,
    interface_coupling,
    leaf_sources,
    parent_sources,
    parent_of,
    update_count,
    update_rows,
):
    inverse = leaf_inv[0, 0]
    parent_inverse = parent_inv[0, 0]
    upward = up_coupling[0, 0]
    downward = down_coupling[0, 0]
    coupling = interface_coupling[0, 0]
    leaf_order = inverse.shape[0]
    parent_order = parent_inverse.shape[0]
    iface_rows = coupling.shape[1]
    parents = parent_of[0]
    counts = update_count[0]
    row_ids = update_rows[0]
    update_cap = row_ids.shape[1]
    myself = lax.axis_index("front")
    slot_ids = jnp.arange(update_cap, dtype=jnp.int32)[None, :]
    live_slots = slot_ids < counts[:, None]
    mine = live_slots & (parents[:, None] == myself)
    targets = jnp.where(mine, row_ids, parent_order).reshape(-1)
    own_live = lax.dynamic_index_in_dim(live_slots, myself, 0, keepdims=False)
    own_rows = lax.dynamic_index_in_dim(row_ids, myself, 0, keepdims=False)
    own_parent = lax.dynamic_index_in_dim(parents, myself, 0, keepdims=False)
    leaf_list = []
    parent_list = []
    previous = None
    for tick_index in range(TICKS):
        sources = leaf_sources[0, 0, tick_index]
        interface = None
        if tick_index > 0:
            interface = passed_along(previous[leaf_order - iface_rows :], "panel", 1)
        partial_solution = product(inverse, sources)
        if interface is not None:
            partial_solution = partial_solution + product(inverse, product(coupling, interface))
        update = jnp.where(own_live[:, None], product(upward, partial_solution), 0.0)
        everyone = lax.all_gather(update, "front", axis=0, tiled=True)
        assembled = jax.ops.segment_sum(everyone, targets, num_segments=parent_order + 1)[
            :parent_order
        ]
        solved = product(parent_inverse, parent_sources[0, 0, tick_index] - assembled)
        all_parents = lax.all_gather(solved, "front", axis=0, tiled=True)
        take_index = own_parent * parent_order + own_rows
        picked = jnp.where(own_live[:, None], jnp.take(all_parents, take_index, axis=0), 0.0)
        leaf_now = partial_solution - product(downward, picked)
        leaf_list.append(leaf_now)
        parent_list.append(solved)
        previous = leaf_now
    leaf_out = jnp.stack(leaf_list, axis=0)[None, None]
    parent_out = jnp.stack(parent_list, axis=0)[None, None]
    return (leaf_out, parent_out)


def solution(mesh):
    placed = (
        P("panel", "front", None, None),
        P("panel", "front", None, None),
        P("panel", "front", None, None),
        P("panel", "front", None, None),
        P("panel", "front", None, None),
        P("panel", "front", None, None, None),
        P("panel", "front", None, None, None),
        P("panel", None),
        P("panel", None),
        P("panel", None, None),
    )
    return jax.shard_map(
        local,
        mesh=mesh,
        in_specs=placed,
        out_specs=(P("panel", "front", None, None, None), P("panel", "front", None, None, None)),
        check_vma=False,
    )
```

profile of v0, /device:TPU:1, one launch (start us, length us, event | category | flops | bytes accessed | tf_op | source)
XLA Modules:
  0.0 501.4 jit_solution(5184536901057421567)
XLA Ops:
  7.2 0.8 compare_bitcast_fusion
  8.0 0.7 iota_compare_fusion
  8.9 3.1 fusion.14
  12.0 0.7 copy-done.5
  12.7 1.8 fusion.60
  14.6 0.8 copy.27
  15.3 0.6 broadcast_select_fusion
  16.0 43.4 %all-gather.7.cloned.1.call-done = f32[6144,128]{1,0:T(8,128)} async-done(((f32[384,128]{1,0:T(8,128)}), f32[6144,128]{1,0:T(8,128)}) %all-gather.7.cloned.1.call-update) | async-done | bytes 3145744 | tf_op jit(solution)/shard_map/all_gather | solution.py:66
  59.4 43.5 %scatter_custom_fusion = f32[769,128]{1,0:T(8,128)} fusion(s32[6144]{0:T(1024)} %bitcast.157, f32[6144,128]{1,0:T(8,128)} %all-gather.7.cloned.1.call-done, f32[]{:T(128)} %constant.34.clone.1), kind=kCustom, calls=%fused_computation.73 | custom fusion | flops 786432 | bytes 394240 | tf_op jit(solution)/shard_map/scatter-add | solution.py:67
  102.9 4.8 fusion.4
  108.4 1.4 add_reduce_fusion
  109.8 43.2 %all-gather.9.cloned.1.call-done = f32[12288,128]{0,1:T(8,128)} async-done(((f32[768,128]{0,1:T(8,128)}), f32[12288,128]{0,1:T(8,128)}) %all-gather.9.cloned.1.call-update) | async-done | bytes 6291472 | tf_op jit(solution)/shard_map/all_gather | solution.py:71
  152.9 6.6 %copy.12 = f32[12288,128]{1,0:T(8,128)} copy(f32[12288,128]{0,1:T(8,128)} %all-gather.9.cloned.1.call-done) | data formatting | bytes 12582912 | tf_op jit(solution)/shard_map/all_gather | solution.py:71
  159.5 4.4 gather_fusion
  163.9 2.6 fusion.29
  166.6 0.8 copy-done.8
  167.4 3.4 collective-permute-start
  170.8 3.0 fusion.12
  173.8 2.2 collective-permute-done
  176.0 1.5 fusion.18
  177.4 2.0 fusion.33
  179.5 0.7 copy-done.7
  180.2 1.8 fusion.57
  182.0 41.1 %all-gather.11.cloned.1.call-done = f32[6144,128]{1,0:T(8,128)} async-done(((f32[384,128]{1,0:T(8,128)}), f32[6144,128]{1,0:T(8,128)}) %all-gather.11.cloned.1.call-update) | async-done | bytes 3145744 | tf_op jit(solution)/shard_map/all_gather | solution.py:66
  223.2 43.5 %scatter_custom_fusion.1 = f32[769,128]{1,0:T(8,128)} fusion(s32[6144]{0:T(1024)} %bitcast.158, f32[6144,128]{1,0:T(8,128)} %all-gather.11.cloned.1.call-done, f32[]{:T(128)} %constant.34.clone.1), kind=kCustom, calls=%fused_computation.71 | custom fusion | flops 786432 | bytes 394240 | tf_op jit(solution)/shard_map/scatter-add | solution.py:67
  266.7 4.8 fusion.2
  271.8 45.0 %all-gather.13.cloned.1.call-done = f32[12288,128]{0,1:T(8,128)} async-done(((f32[768,128]{0,1:T(8,128)}), f32[12288,128]{0,1:T(8,128)}) %all-gather.13.cloned.1.call-update) | async-done | bytes 6291472 | tf_op jit(solution)/shard_map/all_gather | solution.py:71
  316.7 6.6 %copy.15 = f32[12288,128]{1,0:T(8,128)} copy(f32[12288,128]{0,1:T(8,128)} %all-gather.13.cloned.1.call-done) | data formatting | bytes 12582912 | tf_op jit(solution)/shard_map/all_gather | solution.py:71
  323.3 4.4 gather_fusion.1
  327.7 2.6 fusion.28
  330.4 0.7 copy-done.10
  331.1 3.3 collective-permute-start.1
  334.4 3.0 fusion.8
  337.4 2.4 collective-permute-done.1
  339.8 1.5 fusion.16
  341.2 2.0 fusion.30
  343.2 0.7 copy-done.6
  344.0 1.8 fusion.54
  345.8 41.1 %all-gather.15.cloned.1.call-done = f32[6144,128]{1,0:T(8,128)} async-done(((f32[384,128]{1,0:T(8,128)}), f32[6144,128]{1,0:T(8,128)}) %all-gather.15.cloned.1.call-update) | async-done | bytes 3145744 | tf_op jit(solution)/shard_map/all_gather | solution.py:66
  386.9 43.1 %scatter_custom_fusion.2 = f32[769,128]{1,0:T(8,128)S(1)} fusion(s32[6144]{0:T(1024)} %bitcast.159, f32[6144,128]{1,0:T(8,128)} %all-gather.15.cloned.1.call-done, f32[]{:T(128)} %constant.34.clone.1), kind=kCustom, calls=%fused_computation.69 | custom fusion | flops 786432 | bytes 394240 | tf_op jit(solution)/shard_map/scatter-add | solution.py:67
  430.1 4.7 fusion
  434.8 1.3 maximum_bitcast_fusion.1
  436.1 1.4 copy.20
  437.5 42.5 %all-gather.17.cloned.1.call-done = f32[12288,128]{0,1:T(8,128)} async-done(((f32[768,128]{0,1:T(8,128)}), f32[12288,128]{0,1:T(8,128)}) %all-gather.17.cloned.1.call-update) | async-done | bytes 6291472 | tf_op jit(solution)/shard_map/all_gather | solution.py:71
  480.0 6.6 %copy.18 = f32[12288,128]{1,0:T(8,128)} copy(f32[12288,128]{0,1:T(8,128)} %all-gather.17.cloned.1.call-done) | data formatting | bytes 12582912 | tf_op jit(solution)/shard_map/all_gather | solution.py:71
  486.5 4.5 gather_fusion.2
  491.0 2.4 fusion.27
  493.5 1.1 maximum_bitcast_fusion
  (41 shorter events, 1.4 us)
Async XLA Ops:
  7.2 1.7 copy-start
  7.2 52.2 %all-gather.7.cloned.1.call-start = ((), (), s32[]{:S(2)}) async-start(), calls=%async_computation | async-start | bytes 3342336 | tf_op jit(solution)/shard_map/all_gather | solution.py:66
  8.9 3.8 copy-start.1
  11.9 0.7 copy-start.5
  14.5 138.5 %all-gather.9.cloned.1.call-start = ((), (), s32[]{:S(2)}) async-start(), calls=%async_computation.1 | async-start | bytes 6684672 | tf_op jit(solution)/shard_map/all_gather | solution.py:71
  102.9 4.9 copy-start.12
  107.7 115.4 %all-gather.11.cloned.1.call-start = ((), (), s32[]{:S(2)}) async-start(), calls=%async_computation.2 | async-start | bytes 3342336 | tf_op jit(solution)/shard_map/all_gather | solution.py:66
  166.6 0.8 copy-start.8
  167.4 8.6 %copy-start.3 = (f32[1,1,768,512]{3,2,1,0:T(8,128)S(1)}, f32[1,1,768,512]{3,2,1,0:T(8,128)}, u32[]{:S(2)}) copy-start(f32[1,1,768,512]{3,2,1,0:T(8,128)} %param.16) | copy-start | bytes 4718596
  167.4 8.6 %collective-permute-start = (f32[512,128]{1,0:T(8,128)S(1)}, f32[512,128]{1,0:T(8,128)S(1)}, u32[]{:S(2)}, u32[]{:S(2)}) collective-permute-start(f32[512,128]{1,0:T(8,128)S(1)} %slice.51), channel_id=1, source_target_pairs={{0,16},{16,32},{32,48},{48,64},{64,80},{80,96},{96,112},{112,128},... | collective-permute-start | bytes 786440 | tf_op jit(solution)/shard_map/ppermute | solution.py:15
  179.5 0.7 copy-start.7
  182.0 134.7 %all-gather.13.cloned.1.call-start = ((), (), s32[]{:S(2)}) async-start(), calls=%async_computation.3 | async-start | bytes 6684672 | tf_op jit(solution)/shard_map/all_gather | solution.py:71
  271.5 115.4 %all-gather.15.cloned.1.call-start = ((), (), s32[]{:S(2)}) async-start(), calls=%async_computation.4 | async-start | bytes 3342336 | tf_op jit(solution)/shard_map/all_gather | solution.py:66
  330.4 0.7 copy-start.10
  331.1 8.6 %copy-start.4 = (f32[1,1,768,512]{3,2,1,0:T(8,128)S(1)}, f32[1,1,768,512]{3,2,1,0:T(8,128)}, u32[]{:S(2)}) copy-start(f32[1,1,768,512]{3,2,1,0:T(8,128)} %param.16) | copy-start | bytes 4718596
  331.1 8.6 %collective-permute-start.1 = (f32[512,128]{1,0:T(8,128)S(1)}, f32[512,128]{1,0:T(8,128)S(1)}, u32[]{:S(2)}, u32[]{:S(2)}) collective-permute-start(f32[512,128]{1,0:T(8,128)S(1)} %slice.53), channel_id=1, source_target_pairs={{0,16},{16,32},{32,48},{48,64},{64,80},{80,96},{96,112},{112,128},... | collective-permute-start | bytes 786440 | tf_op jit(solution)/shard_map/ppermute | solution.py:15
  343.2 0.7 copy-start.6
  345.8 134.2 %all-gather.17.cloned.1.call-start = ((), (), s32[]{:S(2)}) async-start(), calls=%async_computation.5 | async-start | bytes 6684672 | tf_op jit(solution)/shard_map/all_gather | solution.py:71
  486.5 4.5 copy-start.2
  491.0 2.4 copy-start.9
  491.0 2.4 copy-start.11
Sparse Core Ops, SparseCore 0:
  14.6 44.7 all-gather.6
  107.8 45.0 all-gather.8
  182.1 41.0 all-gather.10
  271.6 45.0 all-gather.12
  345.9 41.0 all-gather.14
  434.9 45.0 all-gather.16
where the time goes:
time: 502 us; the launch traced here: 501 us
  waiting for transfers between devices  261 us (52%)
  other arithmetic  137 us (27%)
  matrix products  43.2 us (9%)
  local copies, waits for them, and re-layouts  39 us (8%)
  between operations  14.3 us (3%)
  starting transfers between devices  7.16 us (1%)
    all_gather x3, waiting for transfers between devices, local(): all_parents = lax.all_gather(solved, 'front', axis=0, tiled=True)  131 us
    scatter-add x3, other arithmetic, local(): jax.ops.segment_sum(everyone, targets, num_segments=parent_order + 1)  130 us
    all_gather x3, waiting for transfers between devices, local(): everyone = lax.all_gather(update, 'front', axis=0, tiled=True)  126 us
    dot_general x16, matrix products, product(): jnp.dot(matrix, operand, precision=highest_precision, preferred_element_t...  43.2 us
    all_gather x3, local copies, waits for them, and re-layouts, local(): all_parents = lax.all_gather(solved, 'front', axis=0, tiled=True)  19.7 us
    gather x3, local copies, waits for them, and re-layouts, local(): jnp.take(all_parents, take_index, axis=0)  13.3 us
  transfers between devices with their start and end apart: 8, of which 8 were waited for; matrix products, arithmetic and copies ran while one was open for 2% of the time, Pallas kernels for 0%

commit v1 on v0

v1 whole, which is shorter than its diff:
```python
import functools

import jax
import jax.numpy as jnp
from jax import lax
from jax.experimental import pallas as pl
from jax.experimental.pallas import tpu as pltpu
from jax.sharding import PartitionSpec as P

F32 = jnp.float32
BF16 = jnp.bfloat16
MESH = pl.DeviceIdType.MESH
HALF = 7.1
PERIOD = 4 * HALF


def dot(a, b):
    return jnp.dot(a, b, preferred_element_type=F32)


def split(x):
    hi = x.astype(BF16)
    return hi, (x - hi.astype(F32)).astype(BF16)


def kernel(
    cfg,
    li_hbm, pi_hbm, up_hbm, dn_hbm, ic_hbm, ls_hbm, ps_hbm, par_ref, cnt_ref, row_ref,
    leaf_hbm, par_hbm,
    LI, PI, UP, DN, IC, LS, PS,
    LIh, LIl, PIh, PIl, UPh, UPl, DNh, DNl, ICh, ICl, Mh, Ml, M2h, M2l,
    V, W, S, T, TG, UB, RB, SB, PXS, PXR, SXS, SXR, XS, XR, ACC, RG, PART, LO, PO,
    ld_sem, st_sem, up_s, up_r, dn_s, dn_r, px_sem, sx_sem, x_s, x_r,
):
    n_panel, n_front, ticks = cfg
    nz = n_front // 2
    dm = nz // 2
    N, C = LS.shape[1:]
    U = UP.shape[0]
    Q = IC.shape[1]
    pr = U // 2
    cr = pr // 2
    hc = C // 2
    panel = lax.axis_index("panel")
    front = lax.axis_index("front")
    z = front // 2
    core = lax.rem(front, 2)
    mate = front + 1 - 2 * core

    def zslot(d):
        return lax.rem(z + d + nz, nz)

    def zdev(d):
        return {"front": 2 * zslot(d) + core}

    ins = [(li_hbm.at[0, 0], LI), (ls_hbm.at[0, 0, 0], LS.at[0]), (up_hbm.at[0, 0], UP), (ps_hbm.at[0, 0], PS)]
    ins += [(pi_hbm.at[0, 0], PI), (ic_hbm.at[0, 0], IC), (ls_hbm.at[0, 0, 1:], LS.at[1:]), (dn_hbm.at[0, 0], DN)]
    loads = [pltpu.make_async_copy(src, dst, ld_sem.at[i]) for i, (src, dst) in enumerate(ins)]
    for c in loads:
        c.start()
    barrier = pltpu.get_barrier_semaphore()
    for who in (
        zdev(1), zdev(-1), {"front": mate},
        {"panel": lax.rem(panel + 1, n_panel)}, {"panel": lax.rem(panel + n_panel - 1, n_panel)},
    ):
        pl.semaphore_signal(barrier, inc=1, device_id=who, device_id_type=MESH)

    def low(shape):
        return lax.broadcasted_iota(jnp.int32, shape, 1) < hc

    def swap(x):
        return pltpu.roll(x, hc, 1)

    def half(x, h):
        return jnp.where(low(x.shape), x, swap(x)) if h == 0 else jnp.where(low(x.shape), swap(x), x)

    def pack(x):
        m = x.shape[0] // 2
        return jnp.where(low((m, C)), x[:m], x[m:])

    def unpack(p):
        m, s = low(p.shape), swap(p)
        return jnp.concatenate([jnp.where(m, p, s), jnp.where(m, s, p)], axis=0)

    def hilo(x):
        hi = x.astype(BF16).astype(F32)
        return jnp.where(low(x.shape), hi, x - hi)

    def fin(o):
        return o + swap(o)

    def mm3(ah, al, x):
        return fin(dot(ah, hilo(x).astype(BF16)) + dot(al, jnp.where(low(x.shape), x, 0.0).astype(BF16)))

    def mm3_full(ah, al, x):
        xh, xl = split(x)
        o = dot(ah, jnp.concatenate([xh, xl], axis=1))
        return o[:, :C] + o[:, C:] + dot(al, xh)

    def mmm(ah, al, bh, bl):
        return dot(ah, bh) + dot(ah, bl) + dot(al, bh)

    def store2(x, hi, lo):
        h, l = split(x)
        hi[...] = h
        lo[...] = l

    def in_half(d, c):
        return c == d

    def chunks(k, c):
        return [d for d in range(2) if k < dm - 1 or in_half(d, c)]

    def up_copy(h, d, k, c, back=0):
        sgn = 1 if d == 0 else -1
        ref = UB.at[h, zslot(-sgn * (k + back)), pl.ds(c * cr, cr)]
        return pltpu.make_async_remote_copy(
            ref, ref, up_s.at[h, d, k, c], up_r.at[h, d, k, c], device_id=zdev(sgn), device_id_type=MESH
        )

    def dn_copy(h, d, k, c):
        at = pl.ds(c * cr, cr)
        return pltpu.make_async_remote_copy(
            SB.at[h, d, k, at], RB.at[h, d, k, at], dn_s.at[h, d, k, c], dn_r.at[h, d, k, c],
            device_id=zdev(1 if d == 0 else -1), device_id_type=MESH,
        )

    def mate_copy(src, dst, sem, h):
        return pltpu.make_async_remote_copy(
            src.at[h], dst.at[h], sem.at[h, 0], sem.at[h, 1], device_id={"front": mate}, device_id_type=MESH
        )

    def x_copy(h, t):
        return pltpu.make_async_remote_copy(
            XS.at[h], XR.at[h, t], x_s.at[h], x_r.at[h, t],
            device_id={"panel": lax.rem(panel + 1, n_panel)}, device_id_type=MESH,
        )

    def all_sends(copy, h):
        for k in range(dm):
            for c in range(2):
                for d in chunks(k, c):
                    copy(h, d, k, c).wait_send()

    def out_copy(src, dst, i, t):
        return pltpu.make_async_copy(src.at[t], dst.at[0, 0, t], st_sem.at[i, t])

    def share(h, k):
        w = zslot(k)
        par = jnp.full((1, C), par_ref[0, 2 * w + core], jnp.int32)
        r = hilo(unpack(UB[h, w]))
        both = [jnp.where(par == who, r, 0.0).astype(BF16) for who in (front, mate)]
        return dot(S[w], jnp.concatenate(both, axis=1))

    def sel(h, k):
        w = zslot(k)
        par = par_ref[0, 2 * w + core]
        which = jnp.where(par == front, 0, jnp.where(par == mate, 1, 2))
        return pack(fin(dot(T[w], RG[h, which])))

    def start(h):
        for c in range(2):
            for d in range(2):
                up_copy(h, d, 0, c).start()

    def relay(h, k, c):
        for d in chunks(k - 1, c):
            up_copy(h, d, k - 1, c, back=1).wait_recv()
            if k < dm and (k < dm - 1 or in_half(d, c)):
                up_copy(h, d, k, c).start()

    def gather(h, k):
        if k == 0:
            ACC[h] = share(h, 0)
        elif k < dm:
            ACC[h] += share(h, -k) + share(h, k)
        else:
            ACC[h] += share(h, k)

    def arrived(h, t):
        return jnp.where(panel > 0, unpack(XR[h, t - 1]), 0.0)

    def partial(h, t):
        @pl.when(t == 0)
        def _():
            PART[h] = half(V[0], h)

        @pl.when(t > 0)
        def _():
            PART[h] = half(V[t], h) + mm3(Mh[...], Ml[...], arrived(h, t))

    def give(h, t):
        @pl.when(t > 0)
        def _():
            mate_copy(PXS, PXR, px_sem, h).wait_send()
        PXS[h] = pack(fin(ACC[h, :, C:]))
        mate_copy(PXS, PXR, px_sem, h).start()

    def solve(h, t):
        rhs = half(PS[t], h) - fin(ACC[h, :, :C])
        mate_copy(PXS, PXR, px_sem, h).wait_recv()
        solved = mm3(PIh[...], PIl[...], rhs - unpack(PXR[h]))

        @pl.when(t > 0)
        def _():
            mate_copy(SXS, SXR, sx_sem, h).wait_send()
        SXS[h] = pack(solved)
        mate_copy(SXS, SXR, sx_sem, h).start()
        RG[h, 0] = hilo(solved).astype(BF16)
        PO[t, :, h * hc : (h + 1) * hc] = solved[:, h * hc : (h + 1) * hc]
        if h == 1:
            out_copy(PO, par_hbm, 1, t).start()

    def descend(h, t):
        all_sends(up_copy, h)

        @pl.when(t > 0)
        def _():
            all_sends(dn_copy, h)
        mate_copy(SXS, SXR, sx_sem, h).wait_recv()
        RG[h, 1] = hilo(unpack(SXR[h])).astype(BF16)
        g = sel(h, dm)
        for d in range(2):
            at = pl.ds(d * cr, cr)
            SB[h, d, dm - 1, at] = g[d * cr : (d + 1) * cr]
            dn_copy(h, d, dm - 1, d).start()

    def own(h, k):
        for d in range(2):
            SB[h, d, k] = sel(h, (k + 1) * (1 if d == 0 else -1))
        if k == dm - 2:
            for d in range(2):
                dn_copy(h, d, k, 1 - d).start()

    def hop(h, k, c):
        at = pl.ds(c * cr, cr)
        for d in chunks(k + 1, c):
            dn_copy(h, d, k + 1, c).wait_recv()
            SB[h, d, k, at] += RB[h, d, k + 1, at]
            dn_copy(h, d, k, c).start()

    def leaf(h, t, last):
        g = sel(h, 0)
        for c in range(2):
            for d in range(2):
                dn_copy(h, d, 0, c).wait_recv()
        down = unpack(g + RB[h, 0, 0] + RB[h, 1, 0])
        rest = PART[h, N - Q :] - mm3(DNh[N - Q :], DNl[N - Q :], down)

        def send():
            @pl.when(t > 0)
            def _():
                x_copy(h, t - 1).wait_send()
            XS[h] = pack(rest)
            x_copy(h, t).start()
        if last is None:
            pl.when(t < ticks - 1)(send)
        elif not last:
            send()
        top = PART[h, : N - Q] - mm3(DNh[: N - Q], DNl[: N - Q], down)
        LO[t, : N - Q, h * hc : (h + 1) * hc] = top[:, h * hc : (h + 1) * hc]
        LO[t, N - Q :, h * hc : (h + 1) * hc] = rest[:, h * hc : (h + 1) * hc]
        if h == 1:
            out_copy(LO, leaf_hbm, 0, t).start()

    def update(h, t):
        x_copy(h, t - 1).wait_recv()
        UB[h, z] = pack(half(W[t], h) + mm3(M2h[...], M2l[...], arrived(h, t)))

    def targets():
        k = lax.broadcasted_iota(jnp.int32, (1, U), 1)
        for w in range(nz):
            rows = row_ref[0, pl.ds(2 * w + core, 1), :]
            cnt = jnp.full((1, U), cnt_ref[0, 2 * w + core], jnp.int32)
            TG[pl.ds(w, 1), :] = jnp.where(k < cnt, rows, -1)
        RG[0, 2] = jnp.zeros((N, C), BF16)
        RG[1, 2] = jnp.zeros((N, C), BF16)

    def make_s(k):
        w = zslot(k)
        i = lax.broadcasted_iota(jnp.int32, (N, U), 0)
        S[w] = jnp.where(i == TG[pl.ds(w, 1), :], 1.0, 0.0).astype(BF16)

    def make_t(w):
        col = jnp.transpose(TG[...])[:, w : w + 1]
        i = lax.broadcasted_iota(jnp.int32, (U, N), 1)
        T[w] = jnp.where(i == col, 1.0, 0.0).astype(BF16)

    def ready(i, full, hi, lo):
        loads[i].wait()
        store2(full[...], hi, lo)

    def static(t):
        V[t] = mm3_full(LIh[...], LIl[...], LS[t])
        W[t] = mm3_full(UPh[...], UPl[...], V[t])

    loads[0].wait()
    store2(LI[...], LIh, LIl)
    loads[1].wait()
    V[0] = mm3_full(LIh[...], LIl[...], LS[0])
    ready(2, UP, UPh, UPl)
    W[0] = mm3_full(UPh[...], UPl[...], V[0])
    for h in range(2):
        UB[h, z] = pack(half(W[0], h))
    pl.semaphore_wait(barrier, 5)

    def tick(t, carry):
        steps = []

        def at(when, fn, *args):
            steps.append((when, len(steps), functools.partial(fn, *args)))

        def only(when, cond, fn, *args):
            def run():
                fn(*args)

            def go():
                pl.when(cond)(run)
            steps.append((when, len(steps), go))

        for h in range(2):
            b = HALF * h
            at(b, start, h)
            at(b + 0.05, gather, h, 0)
            at(b + 0.5, partial, h, t)
            for k in range(1, dm + 1):
                for c in range(2):
                    at(b + 1.4 + 2 * (k - 1) + (c + 1 if k < dm else 0.9 + 0.1 * c), relay, h, k, c)
                at(b + 1.4 + 2 * k - (0 if k < dm else 0.9) + 0.05, gather, h, k)
            at(b + 1.4 + 2 * dm, give, h, t)
            at(b + 10.5, solve, h, t)
            at(b + 12.4, descend, h, t)
            b += 12.5
            at(b + 0.1, own, h, dm - 2)
            at(b + 1.0, own, h, 1)
            for c in range(2):
                at(b + 2.3 + 0.1 * c, hop, h, dm - 2, c)
                at(b + 3.4 + c, hop, h, 1, c)
                at(b + 5.4 + c, hop, h, 0, c)
            at(b + 2.5, own, h, 0)
        at(21.3, leaf, 0, t, None)
        only(26.0, t < ticks - 1, update, 0, t + 1)
        only(0.5, t > 0, leaf, 1, t - 1, False)
        only(HALF - 0.1, t > 0, update, 1, t)
        one = t == 0
        only(0.01, one, targets)
        only(0.02, one, make_s, 0)
        for k in range(1, dm):
            only(0.3 + 2 * k, one, make_s, k)
            only(0.3 + 2 * k, one, make_s, -k)
        only(0.3 + 2 * dm, one, make_s, dm)
        only(0.7, one, lambda: (loads[3].wait(), ready(4, PI, PIh, PIl)))
        for w in range(nz):
            only(3.5 + w // 2, one, make_t, w)
        only(4.0, one, lambda: (ready(5, IC, ICh, ICl), loads[6].wait()))
        only(4.1, one, lambda: store2(mmm(LIh[...], LIl[...], ICh[...], ICl[...]), Mh, Ml))
        only(6.9, one, static, 1)
        only(9.0, one, lambda: ready(7, DN, DNh, DNl))
        only(17.0, one, lambda: store2(mmm(UPh[...], UPl[...], Mh[...], Ml[...]), M2h, M2l))
        only(24.0, one, static, 2)
        for _, _, fn in sorted(steps, key=lambda s: s[:2]):
            fn()
        return carry

    lax.fori_loop(0, ticks, tick, 0)
    leaf(1, ticks - 1, True)
    for h in range(2):
        all_sends(dn_copy, h)
        mate_copy(PXS, PXR, px_sem, h).wait_send()
        mate_copy(SXS, SXR, sx_sem, h).wait_send()
        x_copy(h, ticks - 2).wait_send()
    for t in range(ticks):
        out_copy(PO, par_hbm, 1, t).wait()
        out_copy(LO, leaf_hbm, 0, t).wait()


def local(cfg, *args):
    n_panel, n_front, ticks = cfg
    li, pi, up, dn, ic, ls, ps, par, cnt, rows = args
    nz = n_front // 2
    dm = nz // 2
    N, C = ls.shape[3:]
    U = up.shape[2]
    Q = ic.shape[3]
    pr = U // 2
    v = pltpu.VMEM
    dma = pltpu.SemaphoreType.DMA
    scratch = [
        v((N, N), F32), v((N, N), F32), v((U, N), F32), v((N, U), F32), v((N, Q), F32),
        v((ticks, N, C), F32), v((ticks, N, C), F32),
        v((N, N), BF16), v((N, N), BF16), v((N, N), BF16), v((N, N), BF16),
        v((U, N), BF16), v((U, N), BF16), v((N, U), BF16), v((N, U), BF16),
        v((N, Q), BF16), v((N, Q), BF16), v((N, Q), BF16), v((N, Q), BF16), v((U, Q), BF16), v((U, Q), BF16),
        v((ticks, N, C), F32), v((ticks, U, C), F32),
        v((nz, N, U), BF16), v((nz, U, N), BF16), v((nz, U), jnp.int32),
        v((2, nz, pr, C), F32), v((2, 2, dm, pr, C), F32), v((2, 2, dm, pr, C), F32),
        v((2, N // 2, C), F32), v((2, N // 2, C), F32), v((2, N // 2, C), F32), v((2, N // 2, C), F32),
        v((2, Q // 2, C), F32), v((2, ticks - 1, Q // 2, C), F32),
        v((2, N, 2 * C), F32), v((2, 3, N, C), BF16), v((2, N, C), F32),
        v((ticks, N, C), F32), v((ticks, N, C), F32),
        dma((8,)), dma((2, ticks)),
        dma((2, 2, dm, 2)), dma((2, 2, dm, 2)), dma((2, 2, dm, 2)), dma((2, 2, dm, 2)),
        dma((2, 2)), dma((2, 2)), dma((2,)), dma((2, ticks - 1)),
    ]
    hbm = pl.BlockSpec(memory_space=pl.ANY)
    smem = pl.BlockSpec(memory_space=pltpu.SMEM)
    return pl.pallas_call(
        functools.partial(kernel, cfg),
        out_shape=(jax.ShapeDtypeStruct(ls.shape, F32), jax.ShapeDtypeStruct(ps.shape, F32)),
        in_specs=[hbm] * 7 + [smem, smem, pl.BlockSpec(memory_space=pltpu.VMEM)],
        out_specs=(hbm, hbm),
        scratch_shapes=scratch,
        compiler_params=pltpu.CompilerParams(
            collective_id=0, has_side_effects=True, vmem_limit_bytes=62 * 1024 * 1024
        ),
        name="sweep",
    )(*args)


def solution(mesh):
    four = P("panel", "front", None, None)
    five = P("panel", "front", None, None, None)

    def step(*args):
        cfg = (mesh.shape["panel"], mesh.shape["front"], args[5].shape[2])
        return local(cfg, *args)

    return jax.shard_map(
        step,
        mesh=mesh,
        in_specs=(four,) * 5 + (five,) * 2 + (P("panel", None), P("panel", None), P("panel", None, None)),
        out_specs=(five, five),
        check_vma=False,
    )
```

time: 502 us -> 171 us (0.34)
  waiting for transfers between devices: 261 us -> 0 us
  Pallas kernels: 0 us -> 166 us
  other arithmetic: 137 us -> 0 us
  matrix products: 43.2 us -> 0 us
  local copies, waits for them, and re-layouts: 39 us -> 3.47 us
  between operations: 14.3 us -> 0.65 us
  starting transfers between devices: 7.16 us -> 0 us
    all_gather x6 -> x0, waiting for transfers between devices: 256 us -> none  [the longest x3 131 us: local(): all_parents = lax.all_gather(solved, 'front', axis=0, tiled=True)]
    pallas_call x0 -> x1, Pallas kernels: none -> 166 us  [local(): pl.pallas_call(functools.partial(kernel, cfg), out_shape=(jax.ShapeDtypeS...]
    scatter-add x3 -> x0, other arithmetic: 130 us -> none  [local(): jax.ops.segment_sum(everyone, targets, num_segments=parent_order + 1)]
    dot_general x16 -> x0, matrix products: 43.2 us -> none  [product(): jnp.dot(matrix, operand, precision=highest_precision, preferred_element_t...]
    all_gather x3 -> x0, local copies, waits for them, and re-layouts: 19.7 us -> none  [local(): all_parents = lax.all_gather(solved, 'front', axis=0, tiled=True)]
    gather x3 -> x0, local copies, waits for them, and re-layouts: 13.3 us -> none  [local(): jnp.take(all_parents, take_index, axis=0)]
    ppermute x2 -> x0, starting transfers between devices: 6.69 us -> none  [passed_along(): lax.ppermute(value, axis, [(source, source + steps) for source in range(l...]
  transfers between devices with their start and end apart: 8 -> 0, of which waited for: 8 -> 0; matrix products, arithmetic and copies ran while one was open for 2% -> 0% of each run, Pallas kernels for 0% -> 0%
where the time goes in v1:
time: 171 us; the launch traced here: 170 us
  Pallas kernels  166 us (97%)
  local copies, waits for them, and re-layouts  3.47 us (2%)
    pallas_call x1, Pallas kernels, local(): pl.pallas_call(functools.partial(kernel, cfg), out_shape=(jax.ShapeDtypeS...  166 us
    unnamed x4, local copies, waits for them, and re-layouts  3.47 us

profile of v1, /device:TPU:1, one launch (start us, length us, event | category | flops | bytes accessed | tf_op | source)
XLA Modules:
  0.0 169.9 jit_solution(9207959178151065087)
XLA Ops:
  0.6 165.8 %sweep.1 = (f32[1,1,3,768,128]{4,3,2,1,0:T(8,128)}, f32[1,1,3,768,128]{4,3,2,1,0:T(8,128)}) custom-call(f32[1,1,768,768]{3,2,1,0:T(8,128)} %li_hbm.1, f32[1,1,768,768]{3,2,1,0:T(8,128)} %pi_hbm.1, f32[1,1,384,768]{3,2,1,0:T(8,128)} %up_hbm.1, f32[1,1,768,384]{3,2,1,0:T(8,128)} %dn_hbm.1, f32[1,1,768,512]{3,2,1,0:T(8,128)} %ic_hbm.1, ...), custom_call_target="tpu_custom_call" | custom-call | tf_op jit(solution)/shard_map/sweep/pallas_call | solution.py:407
  166.4 0.0 copy-start
  166.4 2.5 %copy.14 = f32[1,1,3,768,128]{4,3,2,1,0:T(8,128)} copy(f32[1,1,3,768,128]{4,3,2,1,0:T(8,128)} %get-tuple-element.4) | data formatting | bytes 2359296
  168.9 0.0 copy-done
  168.9 1.0 copy.15
Async XLA Ops:
  166.4 2.5 %copy-start = (f32[1,1,3,768,128]{4,3,2,1,0:T(8,128)S(1)}, f32[1,1,3,768,128]{4,3,2,1,0:T(8,128)}, u32[]{:S(2)}) copy-start(f32[1,1,3,768,128]{4,3,2,1,0:T(8,128)} %get-tuple-element.5) | copy-start | bytes 3538948

commit v2 on v1

--- a/solution.py
+++ b/solution.py
@@ -10,8 +10,11 @@
 F32 = jnp.float32
 BF16 = jnp.bfloat16
 MESH = pl.DeviceIdType.MESH
-HALF = 7.1
-PERIOD = 4 * HALF
+ORDER = (
+    0, 80, 62, 69, 65, 63, 1, 59, 3, 4, 84, 2, 6, 61, 64, 7, 79, 31, 5, 66, 68, 32, 77, 9, 60, 67, 10, 8, 34, 71, 11,
+    35, 72, 76, 74, 12, 13, 73, 75, 70, 14, 37, 15, 38, 36, 16, 78, 40, 39, 41, 17, 19, 18, 43, 42, 44, 45, 22, 46,
+    85, 23, 47, 24, 48, 25, 52, 49, 21, 20, 53, 26, 50, 54, 51, 27, 81, 55, 56, 33, 28, 29, 83, 57, 82, 58, 30,
+)
 
 
 def dot(a, b):
@@ -29,7 +32,7 @@
     leaf_hbm, par_hbm,
     LI, PI, UP, DN, IC, LS, PS,
     LIh, LIl, PIh, PIl, UPh, UPl, DNh, DNl, ICh, ICl, Mh, Ml, M2h, M2l,
-    V, W, S, T, TG, UB, RB, SB, PXS, PXR, SXS, SXR, XS, XR, ACC, RG, PART, LO, PO,
+    V, W, S, T, TG, UB, RB, SB, PXS, PXR, SXS, SXR, XS, XR, ACC, RG, PART, MINE, DOWN, LO, PO,
     ld_sem, st_sem, up_s, up_r, dn_s, dn_r, px_sem, sx_sem, x_s, x_r,
 ):
     n_panel, n_front, ticks = cfg
@@ -226,6 +229,9 @@
             dn_copy(h, d, dm - 1, d).start()
 
     def own(h, k):
+        if k < 0:
+            MINE[h] = sel(h, 0)
+            return
         for d in range(2):
             SB[h, d, k] = sel(h, (k + 1) * (1 if d == 0 else -1))
         if k == dm - 2:
@@ -240,11 +246,11 @@
             dn_copy(h, d, k, c).start()
 
     def leaf(h, t, last):
-        g = sel(h, 0)
         for c in range(2):
             for d in range(2):
                 dn_copy(h, d, 0, c).wait_recv()
-        down = unpack(g + RB[h, 0, 0] + RB[h, 1, 0])
+        down = unpack(MINE[h] + RB[h, 0, 0] + RB[h, 1, 0])
+        DOWN[h] = down
         rest = PART[h, N - Q :] - mm3(DNh[N - Q :], DNl[N - Q :], down)
 
         def send():
@@ -257,9 +263,11 @@
             pl.when(t < ticks - 1)(send)
         elif not last:
             send()
-        top = PART[h, : N - Q] - mm3(DNh[: N - Q], DNl[: N - Q], down)
-        LO[t, : N - Q, h * hc : (h + 1) * hc] = top[:, h * hc : (h + 1) * hc]
         LO[t, N - Q :, h * hc : (h + 1) * hc] = rest[:, h * hc : (h + 1) * hc]
+
+    def top(h, t):
+        rest = PART[h, : N - Q] - mm3(DNh[: N - Q], DNl[: N - Q], DOWN[h])
+        LO[t, : N - Q, h * hc : (h + 1) * hc] = rest[:, h * hc : (h + 1) * hc]
         if h == 1:
             out_copy(LO, leaf_hbm, 0, t).start()
 
@@ -307,63 +315,61 @@
     def tick(t, carry):
         steps = []
 
-        def at(when, fn, *args):
-            steps.append((when, len(steps), functools.partial(fn, *args)))
-
-        def only(when, cond, fn, *args):
+        def at(fn, *args):
+            steps.append(functools.partial(fn, *args))
+
+        def only(cond, fn, *args):
             def run():
                 fn(*args)
 
             def go():
                 pl.when(cond)(run)
-            steps.append((when, len(steps), go))
-
+            steps.append(go)
+
+        one = t == 0
         for h in range(2):
-            b = HALF * h
-            at(b, start, h)
-            at(b + 0.05, gather, h, 0)
-            at(b + 0.5, partial, h, t)
+            at(start, h)
+            at(gather, h, 0)
+            at(partial, h, t)
             for k in range(1, dm + 1):
-                for c in range(2):
-                    at(b + 1.4 + 2 * (k - 1) + (c + 1 if k < dm else 0.9 + 0.1 * c), relay, h, k, c)
-                at(b + 1.4 + 2 * k - (0 if k < dm else 0.9) + 0.05, gather, h, k)
-            at(b + 1.4 + 2 * dm, give, h, t)
-            at(b + 10.5, solve, h, t)
-            at(b + 12.4, descend, h, t)
-            b += 12.5
-            at(b + 0.1, own, h, dm - 2)
-            at(b + 1.0, own, h, 1)
-            for c in range(2):
-                at(b + 2.3 + 0.1 * c, hop, h, dm - 2, c)
-                at(b + 3.4 + c, hop, h, 1, c)
-                at(b + 5.4 + c, hop, h, 0, c)
-            at(b + 2.5, own, h, 0)
-        at(21.3, leaf, 0, t, None)
-        only(26.0, t < ticks - 1, update, 0, t + 1)
-        only(0.5, t > 0, leaf, 1, t - 1, False)
-        only(HALF - 0.1, t > 0, update, 1, t)
-        one = t == 0
-        only(0.01, one, targets)
-        only(0.02, one, make_s, 0)
-        for k in range(1, dm):
-            only(0.3 + 2 * k, one, make_s, k)
-            only(0.3 + 2 * k, one, make_s, -k)
-        only(0.3 + 2 * dm, one, make_s, dm)
-        only(0.7, one, lambda: (loads[3].wait(), ready(4, PI, PIh, PIl)))
+                at(relay, h, k, 0)
+                at(relay, h, k, 1)
+                at(gather, h, k)
+            at(give, h, t)
+            at(solve, h, t)
+            at(descend, h, t)
+            for k in range(dm - 2, -2, -1):
+                at(own, h, k)
+            for k in range(dm - 2, -1, -1):
+                at(hop, h, k, 0)
+                at(hop, h, k, 1)
+            if h == 0:
+                at(leaf, 0, t, None)
+                at(top, 0, t)
+                only(t < ticks - 1, update, 0, t + 1)
+            else:
+                only(t > 0, leaf, 1, t - 1, False)
+                only(t > 0, top, 1, t - 1)
+                only(t > 0, update, 1, t)
+        only(one, targets)
+        for k in (0, 1, -1, 2, -2, 3, -3, 4):
+            only(one, make_s, k)
         for w in range(nz):
-            only(3.5 + w // 2, one, make_t, w)
-        only(4.0, one, lambda: (ready(5, IC, ICh, ICl), loads[6].wait()))
-        only(4.1, one, lambda: store2(mmm(LIh[...], LIl[...], ICh[...], ICl[...]), Mh, Ml))
-        only(6.9, one, static, 1)
-        only(9.0, one, lambda: ready(7, DN, DNh, DNl))
-        only(17.0, one, lambda: store2(mmm(UPh[...], UPl[...], Mh[...], Ml[...]), M2h, M2l))
-        only(24.0, one, static, 2)
-        for _, _, fn in sorted(steps, key=lambda s: s[:2]):
-            fn()
+            only(one, make_t, w)
+        only(one, lambda: (loads[3].wait(), ready(4, PI, PIh, PIl)))
+        only(one, lambda: (ready(5, IC, ICh, ICl), loads[6].wait()))
+        only(one, lambda: store2(mmm(LIh[...], LIl[...], ICh[...], ICl[...]), Mh, Ml))
+        only(one, lambda: store2(mmm(UPh[...], UPl[...], Mh[...], Ml[...]), M2h, M2l))
+        only(one, static, 1)
+        only(one, static, 2)
+        only(one, lambda: ready(7, DN, DNh, DNl))
+        for i in ORDER:
+            steps[i]()
         return carry
 
     lax.fori_loop(0, ticks, tick, 0)
     leaf(1, ticks - 1, True)
+    top(1, ticks - 1)
     for h in range(2):
         all_sends(dn_copy, h)
         mate_copy(PXS, PXR, px_sem, h).wait_send()
@@ -396,7 +402,7 @@
         v((2, nz, pr, C), F32), v((2, 2, dm, pr, C), F32), v((2, 2, dm, pr, C), F32),
         v((2, N // 2, C), F32), v((2, N // 2, C), F32), v((2, N // 2, C), F32), v((2, N // 2, C), F32),
         v((2, Q // 2, C), F32), v((2, ticks - 1, Q // 2, C), F32),
-        v((2, N, 2 * C), F32), v((2, 3, N, C), BF16), v((2, N, C), F32),
+        v((2, N, 2 * C), F32), v((2, 3, N, C), BF16), v((2, N, C), F32), v((2, pr, C), F32), v((2, U, C), F32),
         v((ticks, N, C), F32), v((ticks, N, C), F32),
         dma((8,)), dma((2, ticks)),
         dma((2, 2, dm, 2)), dma((2, 2, dm, 2)), dma((2, 2, dm, 2)), dma((2, 2, dm, 2)),

time: 171 us -> 156 us (0.912)
  Pallas kernels: 166 us -> 150 us
    pallas_call x1, Pallas kernels: 166 us -> 150 us  [local(): pl.pallas_call(functools.partial(kernel, cfg), out_shape=(jax.ShapeDtypeS...]
where the time goes in v2:
time: 156 us; the launch traced here: 154 us
  Pallas kernels  150 us (96%)
  local copies, waits for them, and re-layouts  3.47 us (2%)
    pallas_call x1, Pallas kernels, local(): pl.pallas_call(functools.partial(kernel, cfg), out_shape=(jax.ShapeDtypeS...  150 us
    unnamed x4, local copies, waits for them, and re-layouts  3.47 us

profile of v2, /device:TPU:1, one launch (start us, length us, event | category | flops | bytes accessed | tf_op | source)
XLA Modules:
  0.0 154.1 jit_solution(9198319165623399376)
XLA Ops:
  0.6 150.0 %sweep.1 = (f32[1,1,3,768,128]{4,3,2,1,0:T(8,128)}, f32[1,1,3,768,128]{4,3,2,1,0:T(8,128)}) custom-call(f32[1,1,768,768]{3,2,1,0:T(8,128)} %li_hbm.1, f32[1,1,768,768]{3,2,1,0:T(8,128)} %pi_hbm.1, f32[1,1,384,768]{3,2,1,0:T(8,128)} %up_hbm.1, f32[1,1,768,384]{3,2,1,0:T(8,128)} %dn_hbm.1, f32[1,1,768,512]{3,2,1,0:T(8,128)} %ic_hbm.1, ...), custom_call_target="tpu_custom_call" | custom-call | tf_op jit(solution)/shard_map/sweep/pallas_call | solution.py:413
  150.6 0.0 copy-start
  150.6 2.5 %copy.14 = f32[1,1,3,768,128]{4,3,2,1,0:T(8,128)} copy(f32[1,1,3,768,128]{4,3,2,1,0:T(8,128)} %get-tuple-element.4) | data formatting | bytes 2359296
  153.1 0.0 copy-done
  153.1 1.0 copy.15
Async XLA Ops:
  150.6 2.5 %copy-start = (f32[1,1,3,768,128]{4,3,2,1,0:T(8,128)S(1)}, f32[1,1,3,768,128]{4,3,2,1,0:T(8,128)}, u32[]{:S(2)}) copy-start(f32[1,1,3,768,128]{4,3,2,1,0:T(8,128)} %get-tuple-element.5) | copy-start | bytes 3538948

commit v3 on v2

--- a/solution.py
+++ b/solution.py
@@ -11,9 +11,9 @@
 BF16 = jnp.bfloat16
 MESH = pl.DeviceIdType.MESH
 ORDER = (
-    0, 80, 62, 69, 65, 63, 1, 59, 3, 4, 84, 2, 6, 61, 64, 7, 79, 31, 5, 66, 68, 32, 77, 9, 60, 67, 10, 8, 34, 71, 11,
-    35, 72, 76, 74, 12, 13, 73, 75, 70, 14, 37, 15, 38, 36, 16, 78, 40, 39, 41, 17, 19, 18, 43, 42, 44, 45, 22, 46,
-    85, 23, 47, 24, 48, 25, 52, 49, 21, 20, 53, 26, 50, 54, 51, 27, 81, 55, 56, 33, 28, 29, 83, 57, 82, 58, 30,
+    0, 62, 74, 85, 75, 63, 70, 59, 76, 69, 78, 72, 3, 1, 4, 79, 65, 6, 80, 7, 61, 68, 31, 71, 64, 67, 66, 60, 32, 5,
+    9, 10, 8, 34, 84, 35, 11, 12, 13, 14, 37, 15, 73, 77, 38, 16, 40, 36, 41, 17, 39, 18, 43, 42, 44, 45, 22, 46, 23,
+    19, 2, 47, 24, 25, 33, 48, 49, 20, 26, 50, 27, 83, 53, 54, 81, 21, 28, 55, 56, 82, 51, 57, 52, 58, 29, 30,
 )
 
 
@@ -42,7 +42,9 @@
     U = UP.shape[0]
     Q = IC.shape[1]
     pr = U // 2
+    nsub = 2
     cr = pr // 2
+    sr = cr // nsub
     hc = C // 2
     panel = lax.axis_index("panel")
     front = lax.axis_index("front")
@@ -114,17 +116,17 @@
     def chunks(k, c):
         return [d for d in range(2) if k < dm - 1 or in_half(d, c)]
 
-    def up_copy(h, d, k, c, back=0):
+    def up_copy(h, d, k, c, q, back=0):
         sgn = 1 if d == 0 else -1
-        ref = UB.at[h, zslot(-sgn * (k + back)), pl.ds(c * cr, cr)]
+        ref = UB.at[h, zslot(-sgn * (k + back)), pl.ds(c * cr + q * sr, sr)]
         return pltpu.make_async_remote_copy(
-            ref, ref, up_s.at[h, d, k, c], up_r.at[h, d, k, c], device_id=zdev(sgn), device_id_type=MESH
+            ref, ref, up_s.at[h, d, k, nsub * c + q], up_r.at[h, d, k, nsub * c + q], device_id=zdev(sgn), device_id_type=MESH
         )
 
-    def dn_copy(h, d, k, c):
-        at = pl.ds(c * cr, cr)
+    def dn_copy(h, d, k, c, q):
+        at = pl.ds(c * cr + q * sr, sr)
         return pltpu.make_async_remote_copy(
-            SB.at[h, d, k, at], RB.at[h, d, k, at], dn_s.at[h, d, k, c], dn_r.at[h, d, k, c],
+            SB.at[h, d, k, at], RB.at[h, d, k, at], dn_s.at[h, d, k, nsub * c + q], dn_r.at[h, d, k, nsub * c + q],
             device_id=zdev(1 if d == 0 else -1), device_id_type=MESH,
         )
 
@@ -143,7 +145,8 @@
         for k in range(dm):
             for c in range(2):
                 for d in chunks(k, c):
-                    copy(h, d, k, c).wait_send()
+                    for q in range(nsub):
+                        copy(h, d, k, c, q).wait_send()
 
     def out_copy(src, dst, i, t):
         return pltpu.make_async_copy(src.at[t], dst.at[0, 0, t], st_sem.at[i, t])
@@ -164,13 +167,15 @@
     def start(h):
         for c in range(2):
             for d in range(2):
-                up_copy(h, d, 0, c).start()
+                for q in range(nsub):
+                    up_copy(h, d, 0, c, q).start()
 
     def relay(h, k, c):
-        for d in chunks(k - 1, c):
-            up_copy(h, d, k - 1, c, back=1).wait_recv()
-            if k < dm and (k < dm - 1 or in_half(d, c)):
-                up_copy(h, d, k, c).start()
+        for q in range(nsub):
+            for d in chunks(k - 1, c):
+                up_copy(h, d, k - 1, c, q, back=1).wait_recv()
+                if k < dm and (k < dm - 1 or in_half(d, c)):
+                    up_copy(h, d, k, c, q).start()
 
     def gather(h, k):
         if k == 0:
@@ -226,7 +231,8 @@
         for d in range(2):
             at = pl.ds(d * cr, cr)
             SB[h, d, dm - 1, at] = g[d * cr : (d + 1) * cr]
-            dn_copy(h, d, dm - 1, d).start()
+            for q in range(nsub):
+                dn_copy(h, d, dm - 1, d, q).start()
 
     def own(h, k):
         if k < 0:
@@ -236,19 +242,22 @@
             SB[h, d, k] = sel(h, (k + 1) * (1 if d == 0 else -1))
         if k == dm - 2:
             for d in range(2):
-                dn_copy(h, d, k, 1 - d).start()
+                for q in range(nsub):
+                    dn_copy(h, d, k, 1 - d, q).start()
 
     def hop(h, k, c):
-        at = pl.ds(c * cr, cr)
-        for d in chunks(k + 1, c):
-            dn_copy(h, d, k + 1, c).wait_recv()
-            SB[h, d, k, at] += RB[h, d, k + 1, at]
-            dn_copy(h, d, k, c).start()
+        for q in range(nsub):
+            at = pl.ds(c * cr + q * sr, sr)
+            for d in chunks(k + 1, c):
+                dn_copy(h, d, k + 1, c, q).wait_recv()
+                SB[h, d, k, at] += RB[h, d, k + 1, at]
+                dn_copy(h, d, k, c, q).start()
 
     def leaf(h, t, last):
         for c in range(2):
             for d in range(2):
-                dn_copy(h, d, 0, c).wait_recv()
+                for q in range(nsub):
+                    dn_copy(h, d, 0, c, q).wait_recv()
         down = unpack(MINE[h] + RB[h, 0, 0] + RB[h, 1, 0])
         DOWN[h] = down
         rest = PART[h, N - Q :] - mm3(DNh[N - Q :], DNl[N - Q :], down)
@@ -405,7 +414,7 @@
         v((2, N, 2 * C), F32), v((2, 3, N, C), BF16), v((2, N, C), F32), v((2, pr, C), F32), v((2, U, C), F32),
         v((ticks, N, C), F32), v((ticks, N, C), F32),
         dma((8,)), dma((2, ticks)),
-        dma((2, 2, dm, 2)), dma((2, 2, dm, 2)), dma((2, 2, dm, 2)), dma((2, 2, dm, 2)),
+        dma((2, 2, dm, 4)), dma((2, 2, dm, 4)), dma((2, 2, dm, 4)), dma((2, 2, dm, 4)),
         dma((2, 2)), dma((2, 2)), dma((2,)), dma((2, ticks - 1)),
     ]
     hbm = pl.BlockSpec(memory_space=pl.ANY)

time: 156 us -> 153 us (0.981)
  Pallas kernels: 150 us -> 148 us
    pallas_call x1, Pallas kernels: 150 us -> 148 us  [local(): pl.pallas_call(functools.partial(kernel, cfg), out_shape=(jax.ShapeDtypeS...]
where the time goes in v3:
time: 153 us; the launch traced here: 152 us
  Pallas kernels  148 us (97%)
  local copies, waits for them, and re-layouts  3.47 us (2%)
    pallas_call x1, Pallas kernels, local(): pl.pallas_call(functools.partial(kernel, cfg), out_shape=(jax.ShapeDtypeS...  148 us
    unnamed x4, local copies, waits for them, and re-layouts  3.47 us

profile of v3, /device:TPU:1, one launch (start us, length us, event | category | flops | bytes accessed | tf_op | source)
XLA Modules:
  0.0 152.3 jit_solution(841512810724413983)
XLA Ops:
  0.6 148.2 %sweep.1 = (f32[1,1,3,768,128]{4,3,2,1,0:T(8,128)}, f32[1,1,3,768,128]{4,3,2,1,0:T(8,128)}) custom-call(f32[1,1,768,768]{3,2,1,0:T(8,128)} %li_hbm.1, f32[1,1,768,768]{3,2,1,0:T(8,128)} %pi_hbm.1, f32[1,1,384,768]{3,2,1,0:T(8,128)} %up_hbm.1, f32[1,1,768,384]{3,2,1,0:T(8,128)} %dn_hbm.1, f32[1,1,768,512]{3,2,1,0:T(8,128)} %ic_hbm.1, ...), custom_call_target="tpu_custom_call" | custom-call | tf_op jit(solution)/shard_map/sweep/pallas_call | solution.py:422
  148.8 0.0 copy-start
  148.8 2.5 %copy.14 = f32[1,1,3,768,128]{4,3,2,1,0:T(8,128)} copy(f32[1,1,3,768,128]{4,3,2,1,0:T(8,128)} %get-tuple-element.4) | data formatting | bytes 2359296
  151.3 0.0 copy-done
  151.3 1.0 copy.15
Async XLA Ops:
  148.8 2.5 %copy-start = (f32[1,1,3,768,128]{4,3,2,1,0:T(8,128)S(1)}, f32[1,1,3,768,128]{4,3,2,1,0:T(8,128)}, u32[]{:S(2)}) copy-start(f32[1,1,3,768,128]{4,3,2,1,0:T(8,128)} %get-tuple-element.5) | copy-start | bytes 3538948
